TPU v7x, 256 devices: a whole 4x4x8 slice. The times are simulated.
256 devices in a mesh: row: 8 (over x_hi, y), col: 32 (over z, x_lo, core).
Axes of the slice: x: 4 (x_hi: 2, x_lo: 2; x = x_hi * 2 + x_lo), y: 4, z: 8, core: 2. Of those that a mesh axis runs over, the one named last changes fastest.
Arguments:
- samples: float32 [1024, 64, 128], P(('row', 'col')), may hold values from -6 to 6
- omega: float32 [8, 32, 100, 128, 128], P('row', 'col'), may hold values from -0.12 to 2.12
- block_rows: int32 [8, 32, 100], P('row', 'col'), may hold values from -1 to 1023, as said below
- block_cols: int32 [8, 32, 100], P('row', 'col'), may hold values from -1 to 1023, as said below
Outputs:
- omega_next: float32 [8, 32, 100, 128, 128], P('row', 'col')
Inputs may be any that keep to these rules, and one draw needn't show every extreme that they name: `block_rows`: slots 0 to 3 of the device at (a, b) hold the diagonal blocks I = J = (a * 32 + b) * 4 + k in order of k; the other slots hold distinct off-diagonal blocks whose block row lies in a * 1024 / 8 up to (a + 1) * 1024 / 8 - 1 and whose block column J has (J // 4) % 32 = b; live slots come first and -1 fills the rest; some device has all 100 slots live. `block_cols`: -1 exactly where block_rows is -1.
All inputs are finite; a program needn't handle non-finite values.
Results may differ from a plain program's by a relative error of at most 0.0003.
Values sent between devices are 32-bit elements; how exact they have to be, the bound alone decides.
A program may use at most 128 MiB of HBM per device.

v0:
```python
import jax
import jax.numpy as jnp
from jax import lax
from jax.sharding import PartitionSpec as P

ITERS = 2


STEP = 0.5
PENALTY = 0.1


def gradient_blocks(left_totals, right_samples, left_samples, right_totals, sample_count):
    forward = jnp.einsum(
        "snb,snk->sbk", left_totals, right_samples, precision=lax.Precision.HIGHEST
    )
    mirrored = jnp.einsum(
        "snb,snk->sbk", left_samples, right_totals, precision=lax.Precision.HIGHEST
    )
    return (forward + mirrored) * (0.5 / sample_count)


def proximal(current, grad, active, on_diagonal):
    stepped = current - STEP * grad
    eye_mask = jnp.eye(current.shape[-1], dtype=bool)[None] & on_diagonal[:, None, None]
    shrunk = jnp.sign(stepped) * jnp.maximum(jnp.abs(stepped) - STEP * PENALTY, 0.0)
    lifted = 0.5 * (stepped + jnp.sqrt(stepped * stepped + 4.0 * STEP))
    updated = jnp.where(eye_mask, lifted, shrunk)
    return jnp.where(active[:, None, None], updated, 0.0)


def shards(samples, omega, block_rows, block_cols):
    col_count = lax.axis_size("col")
    row_index = lax.axis_index("row")
    slab_blocks = samples.shape[0]
    sample_count = samples.shape[1]
    width = samples.shape[2]
    group_rows = slab_blocks * col_count
    current = omega[0, 0]
    row_ids = block_rows[0, 0]
    col_ids = block_cols[0, 0]
    active = row_ids >= 0
    local_rows = jnp.where(active, row_ids - row_index * group_rows, -1)
    safe_rows = jnp.maximum(local_rows, 0)
    slab_ids = col_ids // slab_blocks
    local_cols = jnp.where(active, slab_ids // col_count * slab_blocks + col_ids % slab_blocks, 0)
    on_diagonal = active & (row_ids == col_ids)
    row_samples = lax.all_gather(samples, "col", axis=0, tiled=True)
    col_samples = lax.all_gather(samples, "row", axis=0, tiled=True)
    picked_cols = col_samples[local_cols]
    picked_rows = row_samples[safe_rows]
    for iteration in range(ITERS):
        products = jnp.einsum("snk,sbk->snb", picked_cols, current, precision=lax.Precision.HIGHEST)
        flattened = products.reshape(products.shape[0], -1)

        def rows_term(offset, length, flattened=flattened):
            selector = (local_rows[None, :] == jnp.arange(length)[:, None]).astype(jnp.float32)
            summed_part = jnp.dot(selector, flattened, precision=lax.Precision.HIGHEST)
            return summed_part.reshape(length, sample_count, width)

        own_totals = lax.psum_scatter(
            rows_term(jnp.int32(0), slab_blocks * lax.axis_size("col")),
            "col",
            scatter_dimension=0,
            tiled=True,
        )
        row_totals = lax.all_gather(own_totals, "col", axis=0, tiled=True)
        col_totals = lax.all_gather(own_totals, "row", axis=0, tiled=True)
        grad = gradient_blocks(
            row_totals[safe_rows], picked_cols, picked_rows, col_totals[local_cols], sample_count
        )
        current = proximal(current, grad, active, on_diagonal)
    return current[None, None]


def solution(mesh):
    return jax.shard_map(
        shards,
        mesh=mesh,
        in_specs=(
            P(("row", "col"), None, None),
            P("row", "col", None, None, None),
            P("row", "col", None),
            P("row", "col", None),
        ),
        out_specs=P("row", "col", None, None, None),
        check_vma=False,
    )
```

profile of v0, /device:TPU:1, one launch (start us, length us, event | category | flops | bytes accessed | tf_op | source)
XLA Modules:
  0.0 751.3 jit_solution(15371741248821138310)
XLA Ops:
  8.7 54.9 %all-gather.7.cloned.1.call-done = f32[32,64,128]{2,1,0:T(8,128)} async-done(((f32[4,64,128]{2,1,0:T(8,128)}), f32[32,64,128]{2,1,0:T(8,128)}) %all-gather.7.cloned.1.call-update) | async-done | bytes 1048592 | tf_op jit(solution)/shard_map/all_gather | solution.py:49
  63.6 2.0 gather_fusion
  65.6 14.8 %fusion.3 = f32[100,64,128]{2,1,0:T(8,128)S(1)} fusion(f32[100,64,128]{2,1,0:T(8,128)S(1)} %gather_fusion, f32[1,1,100,128,128]{4,3,2,1,0:T(8,128)} %param.5), kind=kOutput, calls=%fused_computation.12 | convolution fusion | flops 1258291200 | bytes 13107200 | tf_op jit(solution)/shard_map/snk,sbk->snb/dot_general | solution.py:53
  80.8 4.1 fusion.7
  84.9 4.4 copy.16
  90.2 121.1 %reduce-scatter.3.cloned.1.call-done = f32[4,64,128]{2,1,0:T(8,128)} async-done(((f32[128,64,128]{2,1,0:T(8,128)}), f32[4,64,128]{2,1,0:T(8,128)}) %reduce-scatter.3.cloned.1.call-update) | async-done | bytes 131088 | tf_op jit(solution)/shard_map/reduce_scatter | solution.py:61
  212.3 69.6 %all-gather.11.cloned.1.call-done = f32[128,64,128]{2,1,0:T(8,128)} async-done(((f32[4,64,128]{2,1,0:T(8,128)}), f32[128,64,128]{2,1,0:T(8,128)}) %all-gather.11.cloned.1.call-update) | async-done | bytes 4194320 | tf_op jit(solution)/shard_map/all_gather | solution.py:48
  281.8 4.6 gather_fusion.2
  286.4 47.3 %all-gather.13.cloned.1.call-done = f32[32,64,128]{2,1,0:T(8,128)} async-done(((f32[4,64,128]{2,1,0:T(8,128)}), f32[32,64,128]{2,1,0:T(8,128)}) %all-gather.13.cloned.1.call-update) | async-done | bytes 1048592 | tf_op jit(solution)/shard_map/all_gather | solution.py:68
  333.7 3.6 gather_fusion.3
  337.3 65.5 %all-gather.9.cloned.1.call-done = f32[128,64,128]{2,1,0:T(8,128)} async-done(((f32[4,64,128]{2,1,0:T(8,128)}), f32[128,64,128]{2,1,0:T(8,128)}) %all-gather.9.cloned.1.call-update) | async-done | bytes 4194320 | tf_op jit(solution)/shard_map/all_gather | solution.py:67
  402.8 4.7 gather_fusion.1
  407.5 12.5 %fusion.19 = f32[100,128,128]{2,1,0:T(8,128)S(1)} fusion(f32[100,64,128]{2,1,0:T(8,128)} %gather_fusion.1, f32[100,64,128]{2,1,0:T(8,128)S(1)} %gather_fusion), kind=kOutput, calls=%fused_computation.48 | convolution fusion | flops 1258291200 | bytes 13107200 | tf_op jit(solution)/shard_map/snb,snk->sbk/dot_general | solution.py:14
  420.0 19.4 %fusion = f32[100,128,128]{2,1,0:T(8,128)S(1)} fusion(f32[1,1,100,128,128]{4,3,2,1,0:T(8,128)} %param.5, f32[100,128,128]{2,1,0:T(8,128)S(1)} %fusion.19, pred[100]{0:T(512)(128)(4,1)S(1)} %fusion.18, pred[128,128]{1,0:T(8,128)(4,1)S(1)} %iota_compare_fusion, pred[100]{0:T(512)(128)(4,1)S(1)} %bitcast_and_fusion, f32[100,64,128]{2,1,0:T(8,128)S(1)} %copy-done.1, ...), kind=kOutput, calls=%fused_computation.8 | convolution fusion | flops 1282867200 | bytes 26230984 | tf_op jit(solution)/shard_map/snb,snk->sbk/dot_general | solution.py:17
  439.4 13.0 %fusion.20 = f32[100,64,128]{2,1,0:T(8,128)S(1)} fusion(f32[100,64,128]{2,1,0:T(8,128)S(1)} %gather_fusion, f32[100,128,128]{2,1,0:T(8,128)S(1)} %fusion), kind=kOutput, calls=%fused_computation.49 | convolution fusion | flops 1258291200 | bytes 13107200 | tf_op jit(solution)/shard_map/snk,sbk->snb/dot_general | solution.py:53
  452.8 4.1 fusion.5
  456.9 4.7 copy.18
  461.7 121.0 %reduce-scatter.5.cloned.1.call-done = f32[4,64,128]{2,1,0:T(8,128)} async-done(((f32[128,64,128]{2,1,0:T(8,128)}), f32[4,64,128]{2,1,0:T(8,128)}) %reduce-scatter.5.cloned.1.call-update) | async-done | bytes 131088 | tf_op jit(solution)/shard_map/reduce_scatter | solution.py:61
  583.4 53.3 %all-gather.17.cloned.1.call-done = f32[32,64,128]{2,1,0:T(8,128)} async-done(((f32[4,64,128]{2,1,0:T(8,128)}), f32[32,64,128]{2,1,0:T(8,128)}) %all-gather.17.cloned.1.call-update) | async-done | bytes 1048592 | tf_op jit(solution)/shard_map/all_gather | solution.py:68
  636.8 3.7 gather_fusion.5
  640.5 65.5 %all-gather.15.cloned.1.call-done = f32[128,64,128]{2,1,0:T(8,128)} async-done(((f32[4,64,128]{2,1,0:T(8,128)}), f32[128,64,128]{2,1,0:T(8,128)}) %all-gather.15.cloned.1.call-update) | async-done | bytes 4194320 | tf_op jit(solution)/shard_map/all_gather | solution.py:67
  706.0 4.7 gather_fusion.4
  710.7 12.5 %fusion.21 = f32[100,128,128]{2,1,0:T(8,128)S(1)} fusion(f32[100,64,128]{2,1,0:T(8,128)} %gather_fusion.4, f32[100,64,128]{2,1,0:T(8,128)S(1)} %gather_fusion), kind=kOutput, calls=%fused_computation.50 | convolution fusion | flops 1258291200 | bytes 13107200 | tf_op jit(solution)/shard_map/snb,snk->sbk/dot_general | solution.py:14
  723.2 20.7 %fusion.2 = f32[1,1,100,128,128]{4,3,2,1,0:T(8,128)} fusion(f32[100,128,128]{2,1,0:T(8,128)} %copy-done, f32[100,128,128]{2,1,0:T(8,128)S(1)} %fusion.21, pred[100]{0:T(512)(128)(4,1)S(1)} %fusion.18, pred[128,128]{1,0:T(8,128)(4,1)S(1)} %iota_compare_fusion, pred[100]{0:T(512)(128)(4,1)S(1)} %bitcast_and_fusion, f32[100,64,128]{2,1,0:T(8,128)S(1)} %copy-done.2, ...), kind=kOutput, calls=%fused_computation.10 | convolution fusion | flops 1282867200 | bytes 26230984 | tf_op jit(solution)/shard_map/snb,snk->sbk/dot_general | solution.py:17
  (39 shorter events, 5.4 us)
Async XLA Ops:
  6.5 57.0 %all-gather.7.cloned.1.call-start = ((), (), s32[]{:S(2)}) async-start(), calls=%async_computation.2 | async-start | bytes 1179648 | tf_op jit(solution)/shard_map/all_gather | solution.py:49
  7.3 204.1 %reduce-scatter.3.cloned.1.call-start = ((), (), s32[]{:S(2)}) async-start(), calls=%async_computation.3 | async-start | bytes 4325376 | tf_op jit(solution)/shard_map/reduce_scatter | solution.py:61
  89.4 122.9 %copy-start.5 = (s32[1,1,100]{2,1,0:T(1,128)S(1)}, s32[1,1,100]{2,1,0:T(1,128)}, u32[]{:S(2)}) copy-start(s32[1,1,100]{2,1,0:T(1,128)} %param.6) | copy-start | bytes 1204
  89.4 122.9 %copy-start.6 = (s32[1,1,100]{2,1,0:T(1,128)S(1)}, s32[1,1,100]{2,1,0:T(1,128)}, u32[]{:S(2)}) copy-start(s32[1,1,100]{2,1,0:T(1,128)} %param.7) | copy-start | bytes 1204
  89.4 192.4 %all-gather.11.cloned.1.call-start = ((), (), s32[]{:S(2)}) async-start(), calls=%async_computation.5 | async-start | bytes 4325376 | tf_op jit(solution)/shard_map/all_gather | solution.py:48
  90.1 243.6 %all-gather.13.cloned.1.call-start = ((), (), s32[]{:S(2)}) async-start(), calls=%async_computation.6 | async-start | bytes 1179648 | tf_op jit(solution)/shard_map/all_gather | solution.py:68
  211.3 191.4 %all-gather.9.cloned.1.call-start = ((), (), s32[]{:S(2)}) async-start(), calls=%async_computation.4 | async-start | bytes 4325376 | tf_op jit(solution)/shard_map/all_gather | solution.py:67
  211.9 370.7 %reduce-scatter.5.cloned.1.call-start = ((), (), s32[]{:S(2)}) async-start(), calls=%async_computation.7 | async-start | bytes 4325376 | tf_op jit(solution)/shard_map/reduce_scatter | solution.py:61
  407.5 12.5 %copy-start.1 = (f32[100,64,128]{2,1,0:T(8,128)S(1)}, f32[100,64,128]{2,1,0:T(8,128)}, u32[]{:S(2)}) copy-start(f32[100,64,128]{2,1,0:T(8,128)} %gather_fusion.2) | copy-start | bytes 9830404
  407.5 12.5 %copy-start.4 = (f32[100,64,128]{2,1,0:T(8,128)S(1)}, f32[100,64,128]{2,1,0:T(8,128)}, u32[]{:S(2)}) copy-start(f32[100,64,128]{2,1,0:T(8,128)} %gather_fusion.3) | copy-start | bytes 9830404
  439.4 13.0 %copy-start = (f32[100,128,128]{2,1,0:T(8,128)}, f32[100,128,128]{2,1,0:T(8,128)S(1)}, u32[]{:S(2)}) copy-start(f32[100,128,128]{2,1,0:T(8,128)S(1)} %fusion) | copy-start | bytes 19660804
  461.6 175.1 %all-gather.17.cloned.1.call-start = ((), (), s32[]{:S(2)}) async-start(), calls=%async_computation.9 | async-start | bytes 1179648 | tf_op jit(solution)/shard_map/all_gather | solution.py:68
  582.7 123.3 %all-gather.15.cloned.1.call-start = ((), (), s32[]{:S(2)}) async-start(), calls=%async_computation.8 | async-start | bytes 4325376 | tf_op jit(solution)/shard_map/all_gather | solution.py:67
  710.7 12.5 %copy-start.2 = (f32[100,64,128]{2,1,0:T(8,128)S(1)}, f32[100,64,128]{2,1,0:T(8,128)}, u32[]{:S(2)}) copy-start(f32[100,64,128]{2,1,0:T(8,128)} %gather_fusion.2) | copy-start | bytes 9830404
  710.7 12.5 %copy-start.3 = (f32[100,64,128]{2,1,0:T(8,128)S(1)}, f32[100,64,128]{2,1,0:T(8,128)}, u32[]{:S(2)}) copy-start(f32[100,64,128]{2,1,0:T(8,128)} %gather_fusion.5) | copy-start | bytes 9830404
Sparse Core Ops, SparseCore 0:
  10.0 53.5 all-gather.6
  89.5 121.7 reduce-scatter.2
  213.2 68.5 all-gather.10
  284.3 49.3 all-gather.12
  335.4 67.3 all-gather.8
  461.7 120.8 reduce-scatter.4
  585.3 51.3 all-gather.16
  638.6 67.3 all-gather.14
where the time goes:
time: 760 us; the launch traced here: 751 us
  waiting for transfers between devices  601 us (79%)
  matrix products  101 us (13%)
  local copies, waits for them, and re-layouts  33.3 us (4%)
  between operations  14.1 us (2%)
    reduce_scatter x2, waiting for transfers between devices, shards(): lax.psum_scatter(rows_term(jnp.int32(0), slab_blocks * lax.axis_size('col...  242 us
    all_gather x2, waiting for transfers between devices, shards(): row_totals = lax.all_gather(own_totals, 'col', axis=0, tiled=True)  131 us
    all_gather x2, waiting for transfers between devices, shards(): col_totals = lax.all_gather(own_totals, 'row', axis=0, tiled=True)  101 us
    all_gather x1, waiting for transfers between devices, shards(): row_samples = lax.all_gather(samples, 'col', axis=0, tiled=True)  69.6 us
    all_gather x1, waiting for transfers between devices, shards(): col_samples = lax.all_gather(samples, 'row', axis=0, tiled=True)  54.9 us
    dot_general x2, matrix products, gradient_blocks(): jnp.einsum('snb,snk->sbk', left_samples, right_totals, precision=lax.Prec...  40.1 us
    dot_general x2, matrix products, shards(): jnp.einsum('snk,sbk->snb', picked_cols, current, precision=lax.Precision....  27.8 us
    dot_general x2, matrix products, gradient_blocks(): jnp.einsum('snb,snk->sbk', left_totals, right_samples, precision=lax.Prec...  25 us
  transfers between devices with their start and end apart: 8, of which 8 were waited for; matrix products, arithmetic and copies ran while one was open for 2% of the time, Pallas kernels for 0%

commit v1 on v0

v1 whole, which is shorter than its diff:
```python
import functools

import jax
import jax.numpy as jnp
from jax import lax
from jax.experimental import pallas as pl
from jax.experimental.pallas import tpu as pltpu
from jax.sharding import PartitionSpec as P

ITERS = 2
STEP = 0.5
PENALTY = 0.1

MESH = pl.DeviceIdType.MESH
F32 = jnp.float32
BF16 = jnp.bfloat16

Z = 8
Y = 4
K = 4
N = 64
B = 128
CHUNK = 20


class Place:
    def __init__(self):
        self.a = lax.axis_index("row")
        self.b = lax.axis_index("col")
        b = self.b
        self.z, self.x, self.c = b // 4, (b // 2) % 2, b % 2
        self.h, self.y = self.a // Y, self.a % Y

    def at_z(self, d):
        return (self.z + d + Z) % Z

    def at_y(self, d):
        return (self.y + d + Y) % Y

    def up(self):
        return (self.a, self.at_z(1) * 4 + self.x * 2 + self.c)

    def down(self):
        return (self.a, self.at_z(-1) * 4 + self.x * 2 + self.c)

    def side(self):
        return (self.a, self.z * 4 + (1 - self.x) * 2 + self.c)

    def twin(self):
        return (self.a, self.z * 4 + self.x * 2 + (1 - self.c))

    def north(self):
        return (self.h * Y + self.at_y(1), self.b)

    def south(self):
        return (self.h * Y + self.at_y(-1), self.b)

    def far(self):
        return ((1 - self.h) * Y + self.y, self.b)

    def everyone(self):
        return (self.up(), self.down(), self.side(), self.twin(),
                self.north(), self.south(), self.far())


class Wire:
    def __init__(self, send, recv):
        self.send, self.recv = send, recv
        self.copies = []

    def __call__(self, src, dst, device):
        i = len(self.copies)
        copy = pltpu.make_async_remote_copy(
            src_ref=src, dst_ref=dst, send_sem=self.send.at[i], recv_sem=self.recv.at[i],
            device_id=device, device_id_type=MESH)
        copy.start()
        self.copies.append(copy)
        return copy

    def finish(self):
        for copy in self.copies:
            copy.wait_send()


def greet(me):
    barrier = pltpu.get_barrier_semaphore()
    others = me.everyone()
    for device in others:
        pl.semaphore_signal(barrier, inc=1, device_id=device, device_id_type=MESH)
    pl.semaphore_wait(barrier, len(others))


class Gather:
    def __init__(self, me, wire, full, group):
        self.me, self.wire, self.full, self.group = me, wire, full, group
        self.twins = []
        self.rings = {}
        self.sides = {}
        self.rows = {}

    def part(self, zz, xx, lo, hi):
        return self.full.at[zz, xx, self.me.c, pl.ds(lo, hi - lo)]

    def to_twin(self, zz, xx, lo, hi, src=None):
        ref = self.part(zz, xx, lo, hi)
        self.twins.append(self.wire(ref if src is None else src, ref, self.me.twin()))

    def ring(self, name, d, zz, xx, lo, hi, src=None):
        for way, device in ((1, self.me.up()), (-1, self.me.down())):
            if zz[way] is None:
                continue
            ref = self.part(zz[way], xx, lo, hi)
            self.rings[name, way, d] = self.wire(ref if src is None else src, ref, device)

    def late(self, src=None):
        me = self.me
        ref = self.part(me.z, me.x, 2, 4)
        src = ref if src is None else src
        self.sides["late"] = self.wire(src, ref, me.side())
        self.ring("late", 1, {1: me.z, -1: me.z}, me.x, 2, 4, src)
        self.to_twin(me.z, me.x, 2, 4, src)

    def early(self, src=None):
        me = self.me
        ref = self.part(me.z, me.x, 0, 2)
        src = ref if src is None else src
        self.ring("early", 1, {1: me.z, -1: me.z}, me.x, 0, 2, src)
        self.sides["early", 0] = self.wire(src, ref, me.side())
        self.to_twin(me.z, me.x, 0, 2, src)

    def cross(self):
        me = self.me
        self.sides["late"].wait_recv()
        self.ring("cross", 1, {1: me.z, -1: me.z}, 1 - me.x, 2, 4)
        self.to_twin(me.z, 1 - me.x, 2, 4)

    def onward(self, name, d):
        me = self.me
        xx = 1 - me.x if name == "cross" else me.x
        lo, hi = (0, 2) if name == "early" else (2, 4)
        if d < 4:
            for way in (1, -1):
                self.rings[name, way, d].wait_recv()
                zz = me.at_z(-way * d)
                if d < 3:
                    self.ring(name, d + 1, {way: zz, -way: None}, xx, lo, hi)
                else:
                    mid = lo if way == 1 else lo + 1
                    self.ring(name, 4, {way: zz, -way: None}, xx, mid, mid + 1)
                if name == "early":
                    ref = self.part(zz, xx, lo, hi)
                    self.sides["early", way * d] = self.wire(ref, ref, me.side())
                self.to_twin(zz, xx, lo, hi)
        else:
            for way in (1, -1):
                self.rings[name, way, 4].wait_recv()
            zz = me.at_z(4)
            if name == "early":
                ref = self.part(zz, xx, lo, hi)
                self.sides["early", 4] = self.wire(ref, ref, me.side())
            self.to_twin(zz, xx, lo, hi)

    def sideways(self, d):
        me = self.me
        self.sides["early", d].wait_recv()
        self.to_twin(me.at_z(-d), 1 - me.x, 0, 2)

    def row_start(self, src):
        me = self.me
        ref = self.group.at[me.a]
        self.rows["far"] = self.wire(src, ref, me.far())
        self.rows[0, 1] = self.wire(src, ref, me.north())
        self.rows[0, -1] = self.wire(src, ref, me.south())

    def row_far(self):
        me = self.me
        self.rows["far"].wait_recv()
        ref = self.group.at[(1 - me.h) * Y + me.y]
        self.rows[1, 1] = self.wire(ref, ref, me.north())
        self.rows[1, -1] = self.wire(ref, ref, me.south())

    def row_onward(self, far):
        me = self.me
        hh = 1 - me.h if far else me.h
        for way, device, lo in ((1, me.north(), 0), (-1, me.south(), 2)):
            self.rows[far, way].wait_recv()
            ref = self.group.at[hh * Y + me.at_y(-way), pl.ds(lo, 2)]
            self.rows[far, way, "half"] = self.wire(ref, ref, device)

    def row_end(self):
        for far in (0, 1):
            for way in (1, -1):
                self.rows[far, way, "half"].wait_recv()

    def end(self):
        for copy in self.twins:
            copy.wait_recv()


def gather_rest(gather):
    gather.onward("late", 1)
    gather.cross()
    gather.onward("early", 1)
    gather.row_onward(0)
    gather.row_far()
    gather.sideways(0)
    gather.onward("late", 2)
    gather.onward("cross", 1)
    gather.onward("early", 2)
    gather.sideways(1)
    gather.sideways(-1)
    gather.onward("late", 3)
    gather.row_onward(1)
    gather.onward("cross", 2)
    gather.onward("early", 3)
    gather.sideways(2)
    gather.sideways(-2)
    gather.onward("late", 4)
    gather.onward("cross", 3)
    gather.onward("early", 4)
    gather.sideways(3)
    gather.sideways(-3)
    gather.onward("cross", 4)
    gather.sideways(4)
    gather.row_end()
    gather.end()


def gather_kernel(own, full, group, send, recv):
    me = Place()
    wire = Wire(send, recv)
    greet(me)
    gather = Gather(me, wire, full, group)
    gather.late(own.at[pl.ds(2, 2)])
    gather.early(own.at[pl.ds(0, 2)])
    gather.row_start(own)
    full[me.z, me.x, me.c] = own[...]
    group[me.a] = own[...]
    gather_rest(gather)
    wire.finish()


ORDER = (4, 3, -3, 2, -2, 1, -1, 0)


def reduce_kernel(part, full, group, total, ring, cross, last, send, recv):
    me = Place()
    wire = Wire(send, recv)
    greet(me)
    twin, side, hop = {}, {}, {}
    for d in ORDER:
        zz = me.at_z(d)
        twin[d] = wire(part.at[zz, :, 1 - me.c], total.at[zz], me.twin())

    def merge(d):
        zz = me.at_z(d)
        twin[d].wait_recv()
        total[zz] = total[zz] + part[zz, :, me.c]
        side[d] = wire(total.at[zz, 1 - me.x, pl.ds(2, 2)], cross.at[zz], me.side())

    def crossed(d):
        zz = me.at_z(d)
        side[d].wait_recv()
        total[zz, me.x, 2:4] = total[zz, me.x, 2:4] + cross[zz]

    def column(s):
        return (me.x, 0) if s == 0 else (1 - me.x, 0) if s == 1 else (me.x, 2)

    ways = ((0, 1, me.up()), (1, -1, me.down()))

    def first(s):
        xx, lo = column(s)
        for w, way, device in ways:
            hop[s, w, 0] = wire(total.at[me.at_z(4), xx, pl.ds(lo + w, 1)],
                                ring.at[s, w, 0, pl.ds(w, 1)], device)

    def onward(s, t):
        xx, lo = column(s)
        for w, way, device in ways:
            zz = me.at_z(way * (4 - t))
            hop[s, w, t - 1].wait_recv()
            if t == 1:
                ring[s, w, 0, w] = ring[s, w, 0, w] + total[zz, xx, lo + w]
                ring[s, w, 0, 1 - w] = total[zz, xx, lo + 1 - w]
            else:
                ring[s, w, t - 1] = ring[s, w, t - 1] + total[zz, xx, lo:lo + 2]
            hop[s, w, t] = wire(ring.at[s, w, t - 1], ring.at[s, w, t], device)

    def arrived(s):
        xx, lo = column(s)
        hop[s, 0, 3].wait_recv()
        hop[s, 1, 3].wait_recv()
        return total[me.z, xx, lo:lo + 2] + ring[s, 0, 3] + ring[s, 1, 3]

    merge(4)
    first(1)
    first(0)
    merge(3)
    merge(-3)
    crossed(4)
    first(2)
    merge(2)
    merge(-2)
    onward(1, 1)
    onward(0, 1)
    merge(1)
    merge(-1)
    merge(0)
    crossed(3)
    crossed(-3)
    onward(2, 1)
    onward(1, 2)
    onward(0, 2)
    crossed(2)
    crossed(-2)
    onward(2, 2)
    onward(1, 3)
    onward(0, 3)
    crossed(1)
    crossed(-1)
    onward(2, 3)
    ring[1, 0, 3] = arrived(1)
    swap = wire(ring.at[1, 0, 3], last, me.side())
    crossed(0)
    mine = full.at[me.z, me.x, me.c]
    mine[2:4] = arrived(2)
    gather = Gather(me, wire, full, group)
    gather.late()
    first_half = arrived(0)
    swap.wait_recv()
    mine[0:2] = first_half + last[...]
    gather.early()
    group[me.a] = mine[...]
    gather.row_start(mine)
    gather_rest(gather)
    wire.finish()


COPIES = 128


def gather_call(own):
    return pl.pallas_call(
        gather_kernel,
        name="gather_samples",
        out_shape=(jax.ShapeDtypeStruct((Z, 2, 2, K, N, B), F32),
                   jax.ShapeDtypeStruct((2 * Y, K, N, B), F32)),
        in_specs=[pl.BlockSpec(memory_space=pltpu.VMEM)],
        out_specs=(pl.BlockSpec(memory_space=pltpu.VMEM), pl.BlockSpec(memory_space=pltpu.VMEM)),
        scratch_shapes=[pltpu.SemaphoreType.DMA((COPIES,)), pltpu.SemaphoreType.DMA((COPIES,))],
        compiler_params=pltpu.CompilerParams(collective_id=0, has_side_effects=True),
    )(own)


def reduce_call(part):
    return pl.pallas_call(
        reduce_kernel,
        name="reduce_totals",
        out_shape=(jax.ShapeDtypeStruct((Z, 2, 2, K, N, B), F32),
                   jax.ShapeDtypeStruct((2 * Y, K, N, B), F32)),
        in_specs=[pl.BlockSpec(memory_space=pltpu.VMEM)],
        out_specs=(pl.BlockSpec(memory_space=pltpu.VMEM), pl.BlockSpec(memory_space=pltpu.VMEM)),
        scratch_shapes=[
            pltpu.VMEM((Z, 2, K, N, B), F32),
            pltpu.VMEM((3, 2, 4, 2, N, B), F32),
            pltpu.VMEM((Z, 2, N, B), F32),
            pltpu.VMEM((2, N, B), F32),
            pltpu.SemaphoreType.DMA((COPIES,)),
            pltpu.SemaphoreType.DMA((COPIES,)),
        ],
        compiler_params=pltpu.CompilerParams(collective_id=1, has_side_effects=True),
    )(part)


def split(v):
    high = v.astype(BF16)
    low = (v - high.astype(F32)).astype(BF16)
    return high, low


def slot_ids(rows, cols, s, group_rows):
    row = rows[s]
    col = cols[s]
    live = row >= 0
    local_row = jnp.maximum(row - lax.axis_index("row") * group_rows, 0)
    local_col = jnp.where(live, col // 128 * K + col % K, 0)
    return live, local_row, local_col


def product(picked, block):
    picked_high, picked_low = picked
    block_high, block_low = split(block)
    left = jnp.concatenate([picked_high, picked_high, picked_low], axis=1)
    right = jnp.concatenate([block_high, block_low, block_high], axis=1)
    return lax.dot_general(left, right, (((1,), (1,)), ((), ())), preferred_element_type=F32)


def gradient(row_total, row_sample, col_sample, col_total):
    (wi_h, wi_l), (xi_h, xi_l) = split(row_total), split(row_sample)
    (xj_h, xj_l), (wj_h, wj_l) = col_sample, split(col_total)
    left = jnp.concatenate([wi_h, xi_h, wi_h, xi_h, wi_l, xi_l], axis=0)
    right = jnp.concatenate([xj_h, wj_h, xj_l, wj_l, xj_h, wj_h], axis=0)
    return lax.dot_general(left, right, (((0,), (0,)), ((), ())), preferred_element_type=F32)


def first_kernel(rows, cols, omega, col_samples, partial):
    base = pl.program_id(0) * CHUNK
    group_rows = partial.shape[0]

    @pl.when(pl.program_id(0) == 0)
    def _():
        partial[...] = jnp.zeros_like(partial)

    def one(i, carry):
        live, r, j = slot_ids(rows, cols, base + i, group_rows)
        terms = product(split(col_samples[j]), omega[i])
        partial[r] = partial[r] + terms * jnp.where(live, 1.0, 0.0)
        return carry

    lax.fori_loop(0, CHUNK, one, 0, unroll=4)


def step_kernel(rows, cols, omega, row_samples, col_samples, row_totals, col_totals, out, partial=None):
    base = pl.program_id(0) * CHUNK
    group_rows = row_samples.shape[0]
    scale = STEP * 0.5 / N

    if partial is not None:
        @pl.when(pl.program_id(0) == 0)
        def _():
            partial[...] = jnp.zeros_like(partial)

    def one(i, carry, diagonal=False):
        live, r, j = slot_ids(rows, cols, base + i, group_rows)
        picked = split(col_samples[j])
        grad = gradient(row_totals[r], row_samples[r], picked, col_totals[j])
        stepped = omega[i] - scale * grad
        limit = jnp.where(live, STEP * PENALTY, 3e38)
        new = stepped - jnp.clip(stepped, -limit, limit)
        if diagonal:
            lifted = 0.5 * (stepped + jnp.sqrt(stepped * stepped + 4.0 * STEP))
            eye = (lax.broadcasted_iota(jnp.int32, (B, B), 0)
                   == lax.broadcasted_iota(jnp.int32, (B, B), 1))
            new = jnp.where(eye, lifted, new)
        out[i] = new
        if partial is not None:
            partial[r] = partial[r] + product(picked, new)
        return carry

    @pl.when(pl.program_id(0) == 0)
    def _():
        lax.fori_loop(0, K, functools.partial(one, diagonal=True), 0, unroll=2)
        lax.fori_loop(K, CHUNK, one, 0, unroll=4)

    @pl.when(pl.program_id(0) > 0)
    def _():
        lax.fori_loop(0, CHUNK, one, 0, unroll=4)


def whole(shape):
    return pl.BlockSpec(shape, lambda g, rows, cols: (0,) * len(shape), pipeline_mode=pl.Buffered(1))


def chunked():
    return pl.BlockSpec((CHUNK, B, B), lambda g, rows, cols: (g, 0, 0))


def kept(shape):
    return pl.BlockSpec(shape, lambda g, rows, cols: (0,) * len(shape))


def first_call(rows, cols, omega, col_samples, group_rows):
    return pl.pallas_call(
        first_kernel,
        name="first_terms",
        grid_spec=pltpu.PrefetchScalarGridSpec(
            num_scalar_prefetch=2,
            grid=(omega.shape[0] // CHUNK,),
            in_specs=[chunked(), whole(col_samples.shape)],
            out_specs=kept((group_rows, N, B)),
        ),
        out_shape=jax.ShapeDtypeStruct((group_rows, N, B), F32),
    )(rows, cols, omega, col_samples)


def step_call(rows, cols, omega, row_samples, col_samples, row_totals, col_totals, last):
    outs = [jax.ShapeDtypeStruct(omega.shape, F32)]
    out_specs = [chunked()]
    if not last:
        outs.append(jax.ShapeDtypeStruct(row_samples.shape, F32))
        out_specs.append(kept(row_samples.shape))
    return pl.pallas_call(
        step_kernel,
        name="last_step" if last else "step",
        grid_spec=pltpu.PrefetchScalarGridSpec(
            num_scalar_prefetch=2,
            grid=(omega.shape[0] // CHUNK,),
            in_specs=[chunked()] + [whole(v.shape) for v in (row_samples, col_samples, row_totals, col_totals)],
            out_specs=out_specs,
        ),
        out_shape=outs,
    )(rows, cols, omega, row_samples, col_samples, row_totals, col_totals)


def shards(samples, omega, block_rows, block_cols):
    current = omega[0, 0]
    rows = block_rows.reshape(-1)
    cols = block_cols.reshape(-1)
    full, group = gather_call(samples)
    row_samples = full.reshape(-1, N, B)
    col_samples = group.reshape(-1, N, B)
    partial = first_call(rows, cols, current, col_samples, row_samples.shape[0])
    for iteration in range(ITERS):
        full, group = reduce_call(partial.reshape(Z, 2, 2, K, N, B))
        row_totals = full.reshape(-1, N, B)
        col_totals = group.reshape(-1, N, B)
        outs = step_call(rows, cols, current, row_samples, col_samples, row_totals, col_totals,
                         iteration == ITERS - 1)
        current = outs[0]
        if iteration < ITERS - 1:
            partial = outs[1]
    return current[None, None]


def solution(mesh):
    return jax.shard_map(
        shards,
        mesh=mesh,
        in_specs=(
            P(("row", "col"), None, None),
            P("row", "col", None, None, None),
            P("row", "col", None),
            P("row", "col", None),
        ),
        out_specs=P("row", "col", None, None, None),
        check_vma=False,
    )
```

time: 760 us -> 202 us (0.27); the launches traced: 751 us -> 201 us
  waiting for transfers between devices: 601 us -> 0 us
  Pallas kernels: 0 us -> 201 us
  matrix products: 101 us -> 0 us
  local copies, waits for them, and re-layouts: 33.3 us -> 0 us
  between operations: 14.1 us -> 0.03 us
    all_gather x6 -> x0, waiting for transfers between devices: 356 us -> none  [the longest x2 131 us: shards(): row_totals = lax.all_gather(own_totals, 'col', axis=0, tiled=True)]
    reduce_scatter x2 -> x0, waiting for transfers between devices: 242 us -> none  [shards(): lax.psum_scatter(rows_term(jnp.int32(0), slab_blocks * lax.axis_size('col...]
    pallas_call x0 -> x6, Pallas kernels: none -> 201 us  [the longest x2 105 us: reduce_call(): pl.pallas_call(reduce_kernel, name='reduce_totals', out_shape=(jax.ShapeD...]
    dot_general x8 -> x0, matrix products: 101 us -> none  [the longest x2 40.1 us: gradient_blocks(): jnp.einsum('snb,snk->sbk', left_samples, right_totals, precision=lax.Prec...]
    gather x6 -> x0, local copies, waits for them, and re-layouts: 23.3 us -> none  [the longest x2 9.36 us: shards(): row_totals[safe_rows]]
    dot_general x4 -> x0, local copies, waits for them, and re-layouts: 10 us -> none  [rows_term(): summed_part = jnp.dot(selector, flattened, precision=lax.Precision.HIGHEST)]
  transfers between devices with their start and end apart: 8 -> 0, of which waited for: 8 -> 0; matrix products, arithmetic and copies ran while one was open for 2% -> 0% of each run, Pallas kernels for 0% -> 0%
where the time goes in v1:
time: 202 us; the launch traced here: 201 us
  Pallas kernels  201 us (100%)
    pallas_call x2, Pallas kernels, reduce_call(): pl.pallas_call(reduce_kernel, name='reduce_totals', out_shape=(jax.ShapeD...  105 us
    pallas_call x2, Pallas kernels, step_call(): pl.pallas_call(step_kernel, name='last_step' if last else 'step', grid_sp...  46.5 us
    pallas_call x1, Pallas kernels, gather_call(): pl.pallas_call(gather_kernel, name='gather_samples', out_shape=(jax.Shape...  37.4 us
    pallas_call x1, Pallas kernels, first_call(): pl.pallas_call(first_kernel, name='first_terms', grid_spec=pltpu.Prefetch...  12 us

profile of v1, /device:TPU:1, one launch (start us, length us, event | category | flops | bytes accessed | tf_op | source)
XLA Modules:
  0.0 201.4 jit_solution(8488003682914654454)
XLA Ops:
  0.0 37.4 %gather_samples.1 = (f32[8,2,2,4,64,128]{5,4,3,2,1,0:T(8,128)}, f32[8,4,64,128]{3,2,1,0:T(8,128)}) custom-call(f32[4,64,128]{2,1,0:T(8,128)} %own.1), custom_call_target="tpu_custom_call" | custom-call | tf_op jit(solution)/shard_map/gather_samples/pallas_call | solution.py:343
  37.4 12.0 %first_terms.1 = f32[128,64,128]{2,1,0:T(8,128)} custom-call(s32[100]{0:T(128)} %bitcast.25, s32[100]{0:T(128)} %bitcast.28, f32[100,128,128]{2,1,0:T(8,128)} %bitcast.12, f32[32,64,128]{2,1,0:T(8,128)} %bitcast.17), custom_call_target="tpu_custom_call" | custom-call | tf_op jit(solution)/shard_map/first_terms/pallas_call | solution.py:473
  49.4 52.5 %reduce_totals.2 = (f32[8,2,2,4,64,128]{5,4,3,2,1,0:T(8,128)}, f32[8,4,64,128]{3,2,1,0:T(8,128)}) custom-call(f32[8,2,2,4,64,128]{5,4,3,2,1,0:T(8,128)} %bitcast.14), custom_call_target="tpu_custom_call" | custom-call | tf_op jit(solution)/shard_map/reduce_totals/pallas_call | solution.py:356
  102.0 31.8 %step.1 = (f32[100,128,128]{2,1,0:T(8,128)}, f32[128,64,128]{2,1,0:T(8,128)}) custom-call(s32[100]{0:T(128)} %bitcast.26, s32[100]{0:T(128)} %bitcast.29, f32[100,128,128]{2,1,0:T(8,128)} %bitcast.13, f32[128,64,128]{2,1,0:T(8,128)} %bitcast.15, f32[32,64,128]{2,1,0:T(8,128)} %bitcast.18, f32[128,64,128]{2,1,0:T(8,128)} %bitcast.22, f32[32,64,128]{2,1,0:T(8,128)} %bitcast.24), custom_call_target="tpu_custom_call" | custom-call | tf_op jit(solution)/shard_map/step/pallas_call | solution.py:492
  133.8 52.9 %reduce_totals.3 = (f32[8,2,2,4,64,128]{5,4,3,2,1,0:T(8,128)}, f32[8,4,64,128]{3,2,1,0:T(8,128)}) custom-call(f32[8,2,2,4,64,128]{5,4,3,2,1,0:T(8,128)} %bitcast.20), custom_call_target="tpu_custom_call" | custom-call | tf_op jit(solution)/shard_map/reduce_totals/pallas_call | solution.py:356
  186.7 14.7 %last_step.1 = f32[100,128,128]{2,1,0:T(8,128)} custom-call(s32[100]{0:T(128)} %bitcast.27, s32[100]{0:T(128)} %bitcast.30, f32[100,128,128]{2,1,0:T(8,128)} %get-tuple-element.17.omega, f32[128,64,128]{2,1,0:T(8,128)} %bitcast.16, f32[32,64,128]{2,1,0:T(8,128)} %bitcast.19, f32[128,64,128]{2,1,0:T(8,128)} %bitcast.21, f32[32,64,128]{2,1,0:T(8,128)} %bitcast.23), custom_call_target="tpu_custom_call" | custom-call | tf_op jit(solution)/shard_map/last_step/pallas_call | solution.py:492
